TPU v7x, 32 devices: a whole 2x2x4 slice. The times are simulated.
32 devices in a mesh: groups: 2 (over y), seq: 4 (over z), head: 4 (over x, core).
Axes of the slice: x: 2, y: 2, z: 4, core: 2. Of those that a mesh axis runs over, the one named last changes fastest.
Arguments:
- prefill_query: bfloat16 [1024, 128, 192], P(('groups', 'seq'), 'head'), parts along dimension 0, may hold values from -12 to 12
- prompt_latents: bfloat16 [1024, 576], P(('groups', 'seq', 'head')), parts along dimension 0, may hold values from -6 to 6
- decode_query: bfloat16 [256, 128, 192], P(('groups', 'seq'), 'head'), parts along dimension 0, may hold values from -12 to 12
- sample_latent: bfloat16 [256, 576], P(('groups', 'seq')), parts along dimension 0, may hold values from -6 to 6
- sample_length: int32 [256], P(('groups', 'seq')), parts along dimension 0, may hold values from 128 to 512
- up_key: bfloat16 [128, 128, 512], P('head'), may hold values from -0.5 to 0.5
- up_value: bfloat16 [128, 512, 128], P('head'), may hold values from -0.25 to 0.25
- out_proj: bfloat16 [16384, 7168], P('head', 'seq'), may hold values from -0.046875 to 0.046875
Outputs:
- prefill_heads: bfloat16 [1024, 16384], P(('groups', 'seq'), 'head'), parts along dimension 0
- decode_out: bfloat16 [256, 7168], P(('groups', 'head'), 'seq'), parts along dimension 0
There are 2 independent parts, one for each index of `groups`. A program takes and returns all parts, laid end to end along the dimension named above; an argument that names none is the same for every part. Nothing has to cross between parts.
All inputs are finite; a program needn't handle non-finite values.
Results may differ from a plain program's by a relative error of at most 0.018.
Values may be sent and summed in bfloat16 or wider, within the bound.
A program may use at most 64 MiB of HBM per device.

v0:
```python
import jax
import jax.numpy as jnp
from jax import lax
from jax.sharding import PartitionSpec as P


def absorb(query, up_key, nope_width):
    nope = jnp.einsum(
        "rhn,hnc->rhc", query[:, :, :nope_width], up_key, preferred_element_type=jnp.float32
    )
    return jnp.concatenate([nope.astype(jnp.bfloat16), query[:, :, nope_width:]], axis=2)


def fold_block(state, queries, piece, allowed_fn, kv_width, scale):
    peak, total, summed = state
    key_pos = jnp.arange(piece.shape[0], dtype=jnp.int32)
    allowed = allowed_fn(key_pos)
    scores = (
        lax.dot_general(
            queries, piece, (((1,), (1,)), ((), ())), preferred_element_type=jnp.float32
        )
        * scale
    )
    scores = jnp.where(allowed, scores, -1e30)
    new_peak = jnp.maximum(peak, jnp.max(scores, axis=1))
    weights = jnp.where(allowed, jnp.exp(scores - new_peak[:, None]), 0.0)
    factor = jnp.exp(peak - new_peak)
    total = total * factor + jnp.sum(weights, axis=1)
    summed = summed * factor[:, None] + jnp.dot(
        weights.astype(jnp.bfloat16), piece[:, :kv_width], preferred_element_type=jnp.float32
    )
    return (new_peak, total, summed)


def finish(state, rows, head_count, up_value):
    peak, total, summed = state
    latent = (summed / total[:, None]).astype(jnp.bfloat16).reshape(rows, head_count, -1)
    heads = jnp.einsum("rhc,hcv->rhv", latent, up_value, preferred_element_type=jnp.float32)
    return heads.astype(jnp.bfloat16).reshape(rows, -1)


def per_device(
    prefill_query,
    prompt_latents,
    decode_query,
    sample_latent,
    sample_length,
    up_key,
    up_value,
    out_proj,
):
    local_rows, head_count, query_width = prefill_query.shape
    sample_rows = decode_query.shape[0]
    nope_width = up_key.shape[1]
    kv_width = up_key.shape[2]
    scale = query_width ** (-0.5)
    block = lax.all_gather(prompt_latents, "head", axis=0, tiled=True)
    prefill_rows = absorb(prefill_query, up_key, nope_width).reshape(local_rows * head_count, -1)
    first = lax.axis_index("seq") * local_rows
    query_pos = first + jnp.arange(local_rows * head_count, dtype=jnp.int32) // head_count
    decode_abs = absorb(decode_query, up_key, nope_width)
    decode_rows = decode_abs.reshape(sample_rows * head_count, -1)
    row_length = jnp.repeat(sample_length, head_count)
    own = (
        jnp.einsum(
            "rhc,rc->rh", decode_abs, sample_latent, preferred_element_type=jnp.float32
        ).reshape(-1)
        * scale
    )
    own_values = jnp.repeat(sample_latent[:, :kv_width].astype(jnp.float32), head_count, axis=0)
    count_prefill = local_rows * head_count
    prefill_init = (
        jnp.full((count_prefill,), -1e30, jnp.float32),
        jnp.zeros((count_prefill,), jnp.float32),
        jnp.zeros((count_prefill, kv_width), jnp.float32),
    )
    decode_init = (own, jnp.ones_like(own), own_values)

    def prefill_inner(state, piece):
        return fold_block(
            state,
            prefill_rows,
            piece,
            lambda key_pos: key_pos[None, :] <= query_pos[:, None],
            kv_width,
            scale,
        )

    def decode_inner(state, piece):
        return fold_block(
            state,
            decode_rows,
            piece,
            lambda key_pos: key_pos[None, :] < row_length[:, None],
            kv_width,
            scale,
        )

    def prefill_step(state, piece):
        return prefill_inner(state, piece)

    def decode_step(state, piece):
        return decode_inner(state, piece)

    state = (prefill_init, decode_init)
    piece = lax.all_gather(block, "seq", axis=0, tiled=True)
    prefill_state = prefill_step(state[0], piece)
    decode_state = decode_step(state[1], piece)
    prefill_heads = finish(prefill_state, local_rows, head_count, up_value)
    sample_heads = finish(decode_state, sample_rows, head_count, up_value)
    terms = jnp.dot(
        lax.all_gather(sample_heads, "seq", axis=0, tiled=True),
        out_proj,
        preferred_element_type=jnp.float32,
    )
    decode_out = lax.psum_scatter(
        terms.astype(jnp.bfloat16), "head", scatter_dimension=0, tiled=True
    )
    return (prefill_heads, decode_out)


def solution(mesh):
    in_specs = (
        P(("groups", "seq"), "head", None),
        P(("groups", "seq", "head"), None),
        P(("groups", "seq"), "head", None),
        P(("groups", "seq"), None),
        P(("groups", "seq")),
        P("head", None, None),
        P("head", None, None),
        P("head", "seq"),
    )
    out_specs = (P(("groups", "seq"), "head"), P(("groups", "head"), "seq"))
    return jax.shard_map(
        per_device, mesh=mesh, in_specs=in_specs, out_specs=out_specs, check_vma=False
    )
```

profile of v0, /device:TPU:0, one launch (start us, length us, event | category | flops | bytes accessed | tf_op | source)
XLA Modules:
  0.0 110.1 jit_solution(14324028057335278433)
XLA Ops:
  7.2 0.0 all-gather.2.cloned.1.call-start
  7.2 1.0 slice.24
  8.2 1.0 slice.23
  9.2 6.9 %all_gather.9 = bf16[128,576]{1,0:T(8,128)(2,1)S(1)} all-gather(bf16[32,576]{1,0:T(8,128)(2,1)} %param.9), channel_id=1, replica_groups=mesh['groups'=2,'seq'=4,'head'=4] {'head'}, dimensions={0}, use_global_device_ids=true | all-gather | bytes 184320 | tf_op jit(solution)/shard_map/all_gather | solution.py:57
  16.1 18.7 %all_gather.10 = bf16[512,576]{1,0:T(8,128)(2,1)S(1)} all-gather(bf16[128,576]{1,0:T(8,128)(2,1)S(1)} %all_gather.9), channel_id=1, replica_groups=mesh['groups'=2,'seq'=4,'head'=4] {'seq'}, dimensions={0}, use_global_device_ids=true | all-gather | bytes 737280 | tf_op jit(solution)/shard_map/all_gather | solution.py:106
  34.7 0.7 broadcast_in_dim.41
  35.5 0.1 lt.16
  35.5 0.1 copy.35
  35.6 2.9 %fusion.18 = bf16[32,32,512]{2,0,1:T(8,128)(2,1)S(1)} fusion(bf16[32,128,512]{2,1,0:T(8,128)(2,1)} %param.13, bf16[32,32,128]{2,1,0:T(8,128)(2,1)S(1)} %slice.23), kind=kOutput, calls=%fused_computation.27 | convolution fusion | flops 134742016 | bytes 5505024 | tf_op jit(solution)/shard_map/rhn,hnc->rhc/dot_general | solution.py:8
  38.5 0.1 pad_maximum_fusion.1
  38.7 0.4 copy.25
  39.1 0.5 fusion.33
  39.6 0.1 mul.53
  39.7 1.1 fusion.14
  40.8 0.6 fusion.19
  41.4 1.0 fusion.13
  42.5 0.5 copy-done.1
  43.0 1.1 fusion.21
  44.0 0.7 copy.50
  44.8 0.2 reduce-scatter.2.cloned.1.call-start
  45.1 5.5 %convert_bitcast_fusion = bf16[128,32,512]{0,2,1:T(8,128)(2,1)} fusion(bf16[32,128,512]{2,1,0:T(8,128)(2,1)} %param.13, bf16[128,32,192]{0,2,1:T(8,128)(2,1)S(1)} %copy-done.3), kind=kOutput, calls=%fused_computation.14 | convolution fusion | flops 538968064 | bytes 9437184 | tf_op jit(solution)/shard_map/rhn,hnc->rhc/dot_general | solution.py:8
  50.6 4.9 %pad_maximum_fusion = bf16[128,32,576]{0,2,1:T(8,128)(2,1)} fusion(bf16[128,32,64]{0,2,1:T(8,128)(2,1)S(1)} %slice-done, bf16[128,32,512]{0,2,1:T(8,128)(2,1)} %convert_bitcast_fusion), kind=kLoop, calls=%fused_computation.7 | loop fusion | flops 9437184 | bytes 9437184 | tf_op jit(solution)/shard_map/concatenate | solution.py:11
  55.5 9.0 %copy.20 = bf16[128,32,576]{2,1,0:T(8,128)(2,1)} copy(bf16[128,32,576]{0,2,1:T(8,128)(2,1)} %pad_maximum_fusion) | data formatting | bytes 9437184 | tf_op jit(solution)/shard_map/concatenate | solution.py:11
  64.5 5.6 %fusion = (f32[4096]{0:T(1024)S(1)}, f32[4096,512]{0,1:T(8,128)S(1)}) fusion(s32[4096]{0:T(1024)S(1)} %fusion.35, bf16[4096,576]{1,0:T(8,128)(2,1)} %bitcast.38, bf16[512,576]{1,0:T(8,128)(2,1)S(1)} %all_gather.10), kind=kOutput, calls=%fused_computation.4 | convolution fusion | flops 2424303616 | bytes 13729792 | tf_op jit(solution)/shard_map/dot_general | solution.py:19
  70.2 2.6 %fusion.1 = f32[4096]{0:T(1024)S(1)} fusion(f32[4096,512]{0,1:T(8,128)S(1)} %get-tuple-element.11, f32[4096]{0:T(1024)S(1)} %broadcast_maximum_fusion, s32[4096]{0:T(1024)S(1)} %fusion.35), kind=kLoop, calls=%fused_computation.5 | loop fusion | flops 12578816 | bytes 8437760 | tf_op jit(solution)/shard_map/reduce_sum | solution.py:28
  72.7 0.6 copy-done
  73.4 0.0 all-gather.2.cloned.1.call-done
  73.4 8.4 %convolution_convert_fusion = bf16[128,1792]{1,0:T(8,128)(2,1)} fusion(bf16[128,4096]{1,0:T(8,128)(2,1)} %all-gather.2.cloned.1.call-done, bf16[4096,1792]{1,0:T(8,128)(2,1)} %param.15), kind=kOutput, calls=%fused_computation.16 | convolution fusion | flops 1879277568 | bytes 16187392 | tf_op jit(solution)/shard_map/dot_general | solution.py:111
  81.8 6.3 %divide_convert_fusion = bf16[4096,512]{1,0:T(8,128)(2,1)S(1)} fusion(f32[4096,512]{0,1:T(8,128)} %copy-done, f32[4096]{0:T(1024)S(1)} %get-tuple-element.9, f32[4096]{0:T(1024)S(1)} %broadcast_maximum_fusion, f32[4096]{0:T(1024)S(1)} %get-tuple-element.8, s32[4096]{0:T(1024)S(1)} %fusion.35, bf16[512,576]{1,0:T(8,128)(2,1)S(1)} %all_gather.10), kind=kOutput, calls=%fused_computation | convolution fusion | flops 2166358016 | bytes 13172736 | tf_op jit(solution)/shard_map/dot_general | solution.py:29
  88.2 5.2 %fusion.15 = bf16[32,128,128]{1,2,0:T(8,128)(2,1)S(1)} fusion(bf16[32,512,128]{2,1,0:T(8,128)(2,1)S(1)} %copy-done.2, bf16[128,32,512]{2,1,0:T(8,128)(2,1)S(1)} %bitcast.45), kind=kOutput, calls=%fused_computation.25 | convolution fusion | flops 537395200 | bytes 9437184 | tf_op jit(solution)/shard_map/rhc,hcv->rhv/dot_general | solution.py:38
  93.4 1.3 %copy.28 = bf16[128,4096]{1,0:T(8,128)(2,1)} copy(bf16[128,4096]{0,1:T(8,128)(2,1)S(1)} %bitcast.41) | data formatting | bytes 2097152
  94.7 8.6 %reduce-scatter.2.cloned.1.call-done = bf16[32,1792]{1,0:T(8,128)(2,1)} async-done(((bf16[128,1792]{1,0:T(8,128)(2,1)}), bf16[32,1792]{1,0:T(8,128)(2,1)}) %reduce-scatter.2.cloned.1.call-update) | async-done | bytes 114704 | tf_op jit(solution)/shard_map/reduce_scatter | solution.py:116
  (19 shorter events, 0.1 us)
Async XLA Ops:
  7.2 66.2 %all-gather.2.cloned.1.call-start = ((), (), s32[]{:S(2)}) async-start(), calls=%async_computation.1 | async-start | bytes 1310720 | tf_op jit(solution)/shard_map/all_gather | solution.py:112
  35.6 3.5 %copy-start.4 = (bf16[32,576]{1,0:T(8,128)(2,1)S(1)}, bf16[32,576]{1,0:T(8,128)(2,1)}, u32[]{:S(2)}) copy-start(bf16[32,576]{1,0:T(8,128)(2,1)} %param.11) | copy-start | bytes 110596
  40.8 2.2 %copy-start.1 = (bf16[32,512,128]{2,1,0:T(8,128)(2,1)S(1)}, bf16[32,512,128]{2,1,0:T(8,128)(2,1)}, u32[]{:S(2)}) copy-start(bf16[32,512,128]{2,1,0:T(8,128)(2,1)} %param.14) | copy-start | bytes 12582916
  42.4 2.6 %copy-start.3 = (bf16[128,32,192]{0,2,1:T(8,128)(2,1)S(1)}, bf16[128,32,192]{0,2,1:T(8,128)(2,1)}, u32[]{:S(2)}) copy-start(bf16[128,32,192]{0,2,1:T(8,128)(2,1)} %param.8) | copy-start | bytes 4718596
  44.8 58.5 %reduce-scatter.2.cloned.1.call-start = ((), (), s32[]{:S(2)}) async-start(), calls=%async_computation.2 | async-start | bytes 573440 | tf_op jit(solution)/shard_map/reduce_scatter | solution.py:116
  45.0 5.5 %slice-start = ((bf16[128,32,192]{0,2,1:T(8,128)(2,1)}), bf16[128,32,64]{0,2,1:T(8,128)(2,1)S(1)}, s32[]{:S(2)}) async-start(bf16[128,32,192]{0,2,1:T(8,128)(2,1)} %param.8), calls=%async_computation.3 | async-start | bytes 1048576 | tf_op jit(solution)/shard_map/slice | solution.py:11
  70.1 3.2 %copy-start = (f32[4096,512]{0,1:T(8,128)}, f32[4096,512]{0,1:T(8,128)S(1)}, u32[]{:S(2)}) copy-start(f32[4096,512]{0,1:T(8,128)S(1)} %get-tuple-element.11) | copy-start | bytes 25165828
  81.8 6.3 %copy-start.2 = (bf16[32,512,128]{2,1,0:T(8,128)(2,1)S(1)}, bf16[32,512,128]{2,1,0:T(8,128)(2,1)}, u32[]{:S(2)}) copy-start(bf16[32,512,128]{2,1,0:T(8,128)(2,1)} %param.14) | copy-start | bytes 12582916
Sparse Core Ops, SparseCore 0:
  44.9 28.1 all-gather.1
  82.0 21.2 reduce-scatter.1
where the time goes:
time: 111 us; the launch traced here: 110 us
  matrix products  37.6 us (34%)
  blocking collectives  25.6 us (23%)
  local copies, waits for them, and re-layouts  15.5 us (14%)
  between operations  14.2 us (13%)
  waiting for transfers between devices  8.65 us (8%)
  other arithmetic  8.27 us (7%)
    all_gather x1, blocking collectives, per_device(): piece = lax.all_gather(block, 'seq', axis=0, tiled=True)  18.7 us
    concatenate x2, local copies, waits for them, and re-layouts, absorb(): jnp.concatenate([nope.astype(jnp.bfloat16), query[:, :, nope_width:]], ax...  9.38 us
    reduce_scatter x1, waiting for transfers between devices, per_device(): lax.psum_scatter(terms.astype(jnp.bfloat16), 'head', scatter_dimension=0,...  8.6 us
    dot_general x1, matrix products, per_device(): jnp.dot(lax.all_gather(sample_heads, 'seq', axis=0, tiled=True), out_proj...  8.41 us
    dot_general x2, matrix products, absorb(): jnp.einsum('rhn,hnc->rhc', query[:, :, :nope_width], up_key, preferred_el...  8.38 us
    dot_general x2, matrix products, fold_block(): jnp.dot(weights.astype(jnp.bfloat16), piece[:, :kv_width], preferred_elem...  7.31 us
    all_gather x1, blocking collectives, per_device(): block = lax.all_gather(prompt_latents, 'head', axis=0, tiled=True)  6.9 us
    dot_general x2, matrix products, fold_block(): lax.dot_general(queries, piece, (((1,), (1,)), ((), ())), preferred_eleme...  6.7 us
  transfers between devices with their start and end apart: 2, of which 1 were waited for; matrix products, arithmetic and copies ran while one was open for 37% of the time, Pallas kernels for 0%

commit v1 on v0

--- a/solution.py
+++ b/solution.py
@@ -1,6 +1,10 @@
+import functools
+
 import jax
 import jax.numpy as jnp
 from jax import lax
+from jax.experimental import pallas as pl
+from jax.experimental.pallas import tpu as pltpu
 from jax.sharding import PartitionSpec as P
 
 
@@ -39,7 +43,7 @@
     return heads.astype(jnp.bfloat16).reshape(rows, -1)
 
 
-def per_device(
+def plain_device(
     prefill_query,
     prompt_latents,
     decode_query,
@@ -119,6 +123,428 @@
     return (prefill_heads, decode_out)
 
 
+LANES = 128
+MASKED = -1e30
+BF16 = jnp.bfloat16
+F32 = jnp.float32
+
+
+def round_up(value, unit):
+    return -(-value // unit) * unit
+
+
+def softmax_latent(queries, keys_t, values, bias, scale):
+    rows = queries.shape[0]
+    scores = jnp.dot(queries, keys_t, preferred_element_type=F32)
+    per_head, key_count = bias.shape
+    scores = (scores.reshape(rows // per_head, per_head, key_count) + bias[None]).reshape(
+        rows, key_count
+    )
+    peak = jnp.max(scores, axis=1, keepdims=True)
+    weights = jnp.exp((scores - peak) * scale)
+    total = jnp.sum(weights, axis=1, keepdims=True)
+    summed = jnp.dot(weights.astype(BF16), values, preferred_element_type=F32)
+    return (summed * (1.0 / total)).astype(BF16)
+
+
+def step_kernel(
+    cfg,
+    pq_hbm,
+    lat_hbm,
+    dq_hbm,
+    own_ref,
+    len_ref,
+    upk_hbm,
+    upv_hbm,
+    proj_hbm,
+    out_hbm,
+    dec_ref,
+    pq,
+    dq,
+    lat,
+    upk,
+    upv,
+    proj,
+    nope_rows,
+    rope_rows,
+    pre_abs,
+    dec_abs,
+    keys,
+    keys_t,
+    pre_bias,
+    dec_bias,
+    heads,
+    out,
+    terms,
+    arrived,
+    pq_sem,
+    dq_sem,
+    lat_sem,
+    upk_sem,
+    upv_sem,
+    proj_sem,
+    out_sem,
+    z_send,
+    z_recv,
+    x_send,
+    x_recv,
+    c_send,
+    c_recv,
+    h_send,
+    h_recv,
+    r_send,
+    r_recv,
+):
+    ns, nh, scale = cfg["ns"], cfg["nh"], cfg["scale"]
+    rows, hc, width = pq.shape
+    samples = dq.shape[0]
+    nope, kv = upk.shape[1], upk.shape[2]
+    vdim = upv.shape[2]
+    rope = width - nope
+    lat_width = lat.shape[2]
+    block = lat.shape[1]
+    prompt = ns * nh * block
+    padded = keys.shape[1]
+    nx = nh // 2
+    z, hd = lax.axis_index("seq"), lax.axis_index("head")
+    core_peer = hd + 1 - 2 * lax.rem(hd, 2)
+
+    def seq_peer(d):
+        return lax.rem(z + d, ns)
+
+    def head_peer(d):
+        return lax.rem(hd + d, nh)
+
+    copies = {}
+    copies["pq"] = pltpu.make_async_copy(pq_hbm, pq, pq_sem)
+    copies["dq"] = pltpu.make_async_copy(dq_hbm, dq, dq_sem)
+    me_block = z * nh + hd
+    copies["lat"] = pltpu.make_async_copy(lat_hbm, lat.at[me_block], lat_sem)
+    chunks = cfg["chunks"]
+    per_chunk = hc // chunks
+    copies["lat"].start()
+    copies["pq"].start()
+    copies["dq"].start()
+    upk_copies = [
+        pltpu.make_async_copy(
+            upk_hbm.at[pl.ds(c * per_chunk, per_chunk)],
+            upk.at[pl.ds(c * per_chunk, per_chunk)],
+            upk_sem.at[c],
+        )
+        for c in range(chunks)
+    ]
+    for copy in upk_copies:
+        copy.start()
+    upv_copy = pltpu.make_async_copy(upv_hbm, upv, upv_sem)
+    upv_copy.start()
+    proj_copy = pltpu.make_async_copy(proj_hbm, proj, proj_sem)
+    proj_copy.start()
+
+    barrier = pltpu.get_barrier_semaphore()
+    for d in range(1, ns):
+        pl.semaphore_signal(barrier, inc=1, device_id={"seq": seq_peer(d)})
+    for d in range(1, nh):
+        pl.semaphore_signal(barrier, inc=1, device_id={"head": head_peer(d)})
+    pl.semaphore_wait(barrier, ns + nh - 2)
+
+    sent = []
+
+    def send(src, dst, send_sem, recv_sem, device):
+        copy = pltpu.make_async_remote_copy(
+            src_ref=src, dst_ref=dst, send_sem=send_sem, recv_sem=recv_sem, device_id=device
+        )
+        copy.start()
+        sent.append(copy)
+
+    def received(dst, recv_sem, send_sem, device):
+        pltpu.make_async_remote_copy(
+            src_ref=dst, dst_ref=dst, send_sem=send_sem, recv_sem=recv_sem, device_id=device
+        ).wait_recv()
+
+    def lat_block(d, j):
+        return lax.rem(z - d + ns, ns) * nh + lax.rem(hd - 2 * j + nh, nh)
+
+    def to_core(d, j):
+        slot = lat.at[lat_block(d, j)]
+        send(slot, slot, c_send.at[d, j], c_recv.at[d, j], {"head": core_peer})
+
+    def to_x(d):
+        slot = lat.at[lat_block(d, 0)]
+        for j in range(1, nx):
+            send(slot, slot, x_send.at[d, j], x_recv.at[d, j], {"head": head_peer(2 * j)})
+
+    copies["lat"].wait()
+    mine = lat.at[me_block]
+    order = sorted(range(1, ns), key=lambda d: min(d, ns - d))
+    for d in order:
+        send(mine, mine, z_send.at[d], z_recv.at[d], {"seq": seq_peer(d)})
+    to_x(0)
+    to_core(0, 0)
+
+    def take_z(d):
+        received(lat.at[lat_block(d, 0)], z_recv.at[d], z_send.at[d], {"seq": seq_peer(d)})
+        to_x(d)
+        to_core(d, 0)
+
+    def take_x(d):
+        for j in range(1, nx):
+            received(
+                lat.at[lat_block(d, j)], x_recv.at[d, j], x_send.at[d, j], {"head": core_peer}
+            )
+            to_core(d, j)
+
+    rope_rows[...] = jnp.zeros_like(rope_rows)
+    copies["pq"].wait()
+    copies["dq"].wait()
+
+    def spread(source, base, count):
+        step = 8
+
+        def body(i, carry):
+            piece = source[pl.ds(i * step, step)].astype(F32)
+            at = pl.multiple_of(base * hc + i * step * hc, 8)
+            nope_rows[pl.ds(at, step * hc), :] = piece[:, :, :nope].reshape(step * hc, nope)
+            rope_rows[pl.ds(at, step * hc), 0:rope] = piece[:, :, nope:].reshape(step * hc, rope)
+            return carry
+
+        lax.fori_loop(0, count // step, body, 0)
+
+    spread(pq, 0, rows)
+    spread(dq, rows, samples)
+
+    def absorb_head(h, carry):
+        take = pl.ds(h, rows + samples, stride=hc)
+        plain = nope_rows[take, :].astype(BF16)
+        turned = rope_rows[take, :].astype(BF16)
+        absorbed = jnp.dot(plain, upk[h], preferred_element_type=F32).astype(BF16)
+        at = pl.multiple_of(h * rows, 16)
+        pre_abs[pl.ds(at, rows), 0:kv] = absorbed[:rows]
+        pre_abs[pl.ds(at, rows), kv:padded] = turned[:rows]
+        at = pl.multiple_of(h * samples, 16)
+        dec_abs[pl.ds(at, samples), 0:kv] = absorbed[rows:]
+        dec_abs[pl.ds(at, samples), kv:padded] = turned[rows:]
+        return carry
+
+    pending = [functools.partial(take_z, d) for d in order]
+    pending += [functools.partial(take_x, d) for d in [0] + order]
+    share = -(-len(pending) // max(chunks - 1, 1))
+    for c in range(chunks):
+        upk_copies[c].wait()
+        lax.fori_loop(c * per_chunk, (c + 1) * per_chunk, absorb_head, 0, unroll=2)
+        for action in pending[:share]:
+            action()
+        pending = pending[share:]
+    for action in pending:
+        action()
+
+    key_at = lax.broadcasted_iota(jnp.int32, (rows, prompt), 1)
+    query_at = z * rows + lax.broadcasted_iota(jnp.int32, (rows, prompt), 0)
+    pre_bias[...] = jnp.where(key_at <= query_at, 0.0, MASKED)
+    key_at = lax.broadcasted_iota(jnp.int32, dec_bias.shape, 1)
+    own_at = prompt + lax.broadcasted_iota(jnp.int32, dec_bias.shape, 0)
+    dec_bias[...] = jnp.where((key_at < len_ref[...]) | (key_at == own_at), 0.0, MASKED)
+
+    keys[...] = jnp.zeros_like(keys)
+    keys[prompt : prompt + samples, 0:lat_width] = own_ref[...]
+    for d in range(ns):
+        for j in range(nx):
+            at = lax.rem(z - d + ns, ns) * nh + lax.rem(core_peer - 2 * j + nh, nh)
+            received(lat.at[at], c_recv.at[d, j], c_send.at[d, j], {"head": core_peer})
+    for i in range(ns * nh):
+        keys[i * block : (i + 1) * block, 0:lat_width] = lat[i]
+    keys_t[...] = keys[...].T
+
+    upv_copy.wait()
+    dec_heads = cfg["dec_heads"]
+
+    def decode_group(g, carry):
+        at = pl.multiple_of(g * dec_heads * samples, 16)
+        latent = softmax_latent(
+            dec_abs[pl.ds(at, dec_heads * samples), :],
+            keys_t[...],
+            keys[:, 0:kv],
+            dec_bias[...],
+            scale,
+        )
+        for i in range(dec_heads):
+            h = g * dec_heads + i
+            one = jnp.dot(
+                latent[i * samples : (i + 1) * samples], upv[h], preferred_element_type=F32
+            )
+            heads[z, :, pl.ds(pl.multiple_of(h * vdim, vdim), vdim)] = one.astype(BF16)
+        return carry
+
+    lax.fori_loop(0, hc // dec_heads, decode_group, 0)
+    for d in order:
+        slot = heads.at[z]
+        send(slot, slot, h_send.at[d], h_recv.at[d], {"seq": seq_peer(d)})
+
+    pre_heads = cfg["pre_heads"]
+    groups = hc // pre_heads
+    group_cols = pre_heads * vdim
+
+    def prefill_group(g, carry):
+        at = pl.multiple_of(g * pre_heads * rows, 16)
+        latent = softmax_latent(
+            pre_abs[pl.ds(at, pre_heads * rows), :],
+            keys_t[:, 0:prompt],
+            keys[0:prompt, 0:kv],
+            pre_bias[...],
+            scale,
+        )
+        for i in range(pre_heads):
+            h = g * pre_heads + i
+            one = jnp.dot(latent[i * rows : (i + 1) * rows], upv[h], preferred_element_type=F32)
+            out[:, pl.ds(pl.multiple_of(h * vdim, vdim), vdim)] = one.astype(BF16)
+        return carry
+
+    first = groups // 2
+    half_cols = first * group_cols
+    lax.fori_loop(0, first, prefill_group, 0)
+    front = pltpu.make_async_copy(
+        out.at[:, pl.ds(0, half_cols)], out_hbm.at[:, pl.ds(0, half_cols)], out_sem.at[0]
+    )
+    front.start()
+
+    proj_copy.wait()
+    for d in order:
+        at = lax.rem(z - d + ns, ns)
+        received(heads.at[at], h_recv.at[d], h_send.at[d], {"seq": seq_peer(d)})
+    cols = proj.shape[1]
+    tile = cfg["tile"]
+    share_rows = ns * samples // nh
+
+    def project(n, carry):
+        take = pl.ds(pl.multiple_of(n * tile, tile), tile)
+        left = heads[...].reshape(ns * samples, hc * vdim)
+        term = jnp.dot(left, proj[:, take], preferred_element_type=F32).astype(BF16)
+        terms[:, :, take] = term.reshape(nh, share_rows, tile)
+        return carry
+
+    lax.fori_loop(0, cols // tile, project, 0)
+    for d in range(1, nh):
+        peer = head_peer(d)
+        send(terms.at[peer], arrived.at[d], r_send.at[d], r_recv.at[d], {"head": peer})
+
+    lax.fori_loop(first, groups, prefill_group, 0)
+    back_cols = out.shape[1] - half_cols
+    back = pltpu.make_async_copy(
+        out.at[:, pl.ds(half_cols, back_cols)],
+        out_hbm.at[:, pl.ds(half_cols, back_cols)],
+        out_sem.at[1],
+    )
+    back.start()
+    total = terms[hd].astype(F32)
+    for d in range(1, nh):
+        received(arrived.at[d], r_recv.at[d], r_send.at[d], {"head": core_peer})
+        total = total + arrived[d].astype(F32)
+    dec_ref[...] = total.astype(BF16)
+    front.wait()
+    back.wait()
+    for copy in sent:
+        copy.wait_send()
+
+
+def fused_device(ns, nh, pq, lat, dq, own, length, upk, upv, proj):
+    rows, hc, width = pq.shape
+    samples = dq.shape[0]
+    nope, kv = upk.shape[1:]
+    vdim = upv.shape[2]
+    block, lat_width = lat.shape
+    prompt = ns * nh * block
+    padded = round_up(lat_width, LANES)
+    cols = proj.shape[1]
+    share_rows = ns * samples // nh
+    keys_rows = prompt + round_up(samples, LANES)
+    nx = nh // 2
+    dec_heads = max(1, min(hc, 512 // samples))
+    pre_heads = max(1, min(hc // 2, 512 // rows))
+    cfg = {
+        "ns": ns,
+        "nh": nh,
+        "scale": width ** (-0.5),
+        "chunks": 4,
+        "dec_heads": dec_heads,
+        "pre_heads": pre_heads,
+        "tile": 256 if cols % 256 == 0 else LANES,
+    }
+    hbm = pl.BlockSpec(memory_space=pl.ANY)
+    vmem = pl.BlockSpec(memory_space=pltpu.VMEM)
+    dma = pltpu.SemaphoreType.DMA
+    return pl.pallas_call(
+        functools.partial(step_kernel, cfg),
+        out_shape=(
+            jax.ShapeDtypeStruct((rows, hc * vdim), BF16),
+            jax.ShapeDtypeStruct((share_rows, cols), BF16),
+        ),
+        in_specs=[hbm, hbm, hbm, vmem, vmem, hbm, hbm, hbm],
+        out_specs=(hbm, vmem),
+        scratch_shapes=[
+            pltpu.VMEM((rows, hc, width), BF16),
+            pltpu.VMEM((samples, hc, width), BF16),
+            pltpu.VMEM((ns * nh, block, lat_width), BF16),
+            pltpu.VMEM((hc, nope, kv), BF16),
+            pltpu.VMEM((hc, kv, vdim), BF16),
+            pltpu.VMEM(proj.shape, BF16),
+            pltpu.VMEM(((rows + samples) * hc, nope), F32),
+            pltpu.VMEM(((rows + samples) * hc, LANES), F32),
+            pltpu.VMEM((rows * hc, padded), BF16),
+            pltpu.VMEM((samples * hc, padded), BF16),
+            pltpu.VMEM((keys_rows, padded), BF16),
+            pltpu.VMEM((padded, keys_rows), BF16),
+            pltpu.VMEM((rows, prompt), F32),
+            pltpu.VMEM((samples, keys_rows), F32),
+            pltpu.VMEM((ns, samples, hc * vdim), BF16),
+            pltpu.VMEM((rows, hc * vdim), BF16),
+            pltpu.VMEM((nh, share_rows, cols), BF16),
+            pltpu.VMEM((nh, share_rows, cols), BF16),
+            dma,
+            dma,
+            dma,
+            dma((cfg["chunks"],)),
+            dma,
+            dma,
+            dma((2,)),
+            dma((ns,)),
+            dma((ns,)),
+            dma((ns, nx)),
+            dma((ns, nx)),
+            dma((ns, nx)),
+            dma((ns, nx)),
+            dma((ns,)),
+            dma((ns,)),
+            dma((nh,)),
+            dma((nh,)),
+        ],
+        compiler_params=pltpu.CompilerParams(
+            collective_id=0, has_side_effects=True, vmem_limit_bytes=62 * 1024 * 1024
+        ),
+        name="rollout_step",
+    )(pq, lat, dq, own, length.reshape(samples, 1), upk, upv, proj)
+
+
+def per_device(ns, nh, *args):
+    pq, lat, dq, own, length, upk, upv, proj = args
+    samples, hc = dq.shape[:2]
+    fits = (
+        lat.shape[0] % 16 == 0
+        and nh % 2 == 0
+        and ns > 1
+        and hc % 8 == 0
+        and pq.shape[0] % 16 == 0
+        and samples % 16 == 0
+        and (ns * samples) % (nh * 16) == 0
+        and upk.shape[1] == LANES
+        and upk.shape[2] % LANES == 0
+        and upv.shape[2] == LANES
+        and proj.shape[1] % LANES == 0
+        and (ns * nh * lat.shape[0]) % LANES == 0
+    )
+    if fits:
+        return tuple(fused_device(ns, nh, *args))
+    return plain_device(*args)
+
+
 def solution(mesh):
     in_specs = (
         P(("groups", "seq"), "head", None),
@@ -132,5 +558,8 @@
     )
     out_specs = (P(("groups", "seq"), "head"), P(("groups", "head"), "seq"))
     return jax.shard_map(
-        per_device, mesh=mesh, in_specs=in_specs, out_specs=out_specs, check_vma=False
-    )
+        functools.partial(per_device, mesh.shape["seq"], mesh.shape["head"]),
+        mesh=mesh, in_specs=in_specs,
+        out_specs=out_specs,
+        check_vma=False
+    )

time: 111 us -> 65.6 us (0.59)
  Pallas kernels: 0 us -> 54.9 us
  matrix products: 37.6 us -> 0 us
  blocking collectives: 25.6 us -> 0 us
  between operations: 14.2 us -> 0.64 us
  waiting for transfers between devices: 8.65 us -> 0 us
  other arithmetic: 8.27 us -> 0 us
  local copies, waits for them, and re-layouts: 15.5 us -> 9.7 us
    pallas_call x0 -> x1, Pallas kernels: none -> 54.9 us  [fused_device(): pl.pallas_call(functools.partial(step_kernel, cfg), out_shape=(jax.ShapeD...]
    dot_general x10 -> x0, matrix products: 37.6 us -> none  [the longest x1 8.41 us: per_device(): jnp.dot(lax.all_gather(sample_heads, 'seq', axis=0, tiled=True), out_proj...]
    all_gather x2 -> x0, blocking collectives: 25.6 us -> none  [the longest x1 18.7 us: per_device(): piece = lax.all_gather(block, 'seq', axis=0, tiled=True)]
    concatenate x2 -> x0, local copies, waits for them, and re-layouts: 9.38 us -> none  [absorb(): jnp.concatenate([nope.astype(jnp.bfloat16), query[:, :, nope_width:]], ax...]
    reduce_scatter x1 -> x0, waiting for transfers between devices: 8.6 us -> none  [per_device(): lax.psum_scatter(terms.astype(jnp.bfloat16), 'head', scatter_dimension=0,...]
    unnamed x12 -> x3, local copies, waits for them, and re-layouts: 2.59 us -> 8.36 us
    concatenate x2 -> x0, other arithmetic: 5.07 us -> none  [absorb(): jnp.concatenate([nope.astype(jnp.bfloat16), query[:, :, nope_width:]], ax...]
    reduce_sum x2 -> x0, other arithmetic: 3.16 us -> none  [fold_block(): total = total * factor + jnp.sum(weights, axis=1)]
  transfers between devices with their start and end apart: 2 -> 0, of which waited for: 1 -> 0; matrix products, arithmetic and copies ran while one was open for 37% -> 0% of each run, Pallas kernels for 0% -> 0%
where the time goes in v1:
time: 65.6 us; the launch traced here: 65.3 us
  Pallas kernels  54.9 us (84%)
  local copies, waits for them, and re-layouts  9.7 us (15%)
    pallas_call x1, Pallas kernels, fused_device(): pl.pallas_call(functools.partial(step_kernel, cfg), out_shape=(jax.ShapeD...  54.9 us
    unnamed x3, local copies, waits for them, and re-layouts  8.36 us
    reshape x1, local copies, waits for them, and re-layouts, fused_device(): length.reshape(samples, 1)  1.34 us

profile of v1, /device:TPU:0, one launch (start us, length us, event | category | flops | bytes accessed | tf_op | source)
XLA Modules:
  0.0 65.3 jit_solution(13802052574972414046)
XLA Ops:
  0.6 1.3 %copy.11.len_ref = s32[32,1]{1,0:T(8,128)} copy(s32[32,1]{0,1:T(1,128)} %bitcast.1) | data formatting | bytes 256 | tf_op jit(solution)/shard_map/reshape | solution.py:523
  2.0 4.5 %copy.10.pq_hbm = bf16[128,32,192]{2,1,0:T(8,128)(2,1)} copy(bf16[128,32,192]{0,2,1:T(8,128)(2,1)} %param.8) | data formatting | bytes 3145728 | tf_op args[0]
  6.5 54.9 %rollout_step.1 = (bf16[128,4096]{1,0:T(8,128)(2,1)}, bf16[32,1792]{1,0:T(8,128)(2,1)}) custom-call(bf16[128,32,192]{2,1,0:T(8,128)(2,1)} %copy.10.pq_hbm, bf16[32,576]{1,0:T(8,128)(2,1)} %lat_hbm.1, bf16[32,32,192]{2,1,0:T(8,128)(2,1)} %dq_hbm.1, bf16[32,576]{1,0:T(8,128)(2,1)} %own_ref.1, s32[32,1]{1,0:T(8,128)} %copy.11.len_ref, ...), custom_call_target="tpu_custom_call" | custom-call | tf_op jit(solution)/shard_map/rollout_step/pallas_call | solution.py:474
  61.4 2.3 %copy.14 = bf16[128,4096]{1,0:T(8,128)(2,1)} copy(bf16[128,4096]{1,0:T(8,128)(2,1)} %get-tuple-element.4) | data formatting | bytes 2097152
  63.7 1.6 %copy.15 = bf16[32,1792]{1,0:T(8,128)(2,1)} copy(bf16[32,1792]{1,0:T(8,128)(2,1)} %get-tuple-element.5) | data formatting | bytes 229376

commit v2 on v1

--- a/solution.py
+++ b/solution.py
@@ -196,7 +196,7 @@
     r_recv,
 ):
     ns, nh, scale = cfg["ns"], cfg["nh"], cfg["scale"]
-    rows, hc, width = pq.shape
+    hc, width, rows = pq.shape
     samples = dq.shape[0]
     nope, kv = upk.shape[1], upk.shape[2]
     vdim = upv.shape[2]
@@ -294,35 +294,32 @@
             to_core(d, j)
 
     rope_rows[...] = jnp.zeros_like(rope_rows)
+    pre_abs[:, kv:padded] = jnp.zeros((rows * hc, padded - kv), BF16)
+    copies["dq"].wait()
+    step = 8
+
+    def spread(i, carry):
+        piece = dq[pl.ds(i * step, step)].astype(F32)
+        take = pl.ds(pl.multiple_of(i * step * hc, 8), step * hc)
+        nope_rows[take, :] = piece[:, :, :nope].reshape(step * hc, nope)
+        rope_rows[take, 0:rope] = piece[:, :, nope:].reshape(step * hc, rope)
+        return carry
+
+    lax.fori_loop(0, samples // step, spread, 0)
     copies["pq"].wait()
-    copies["dq"].wait()
-
-    def spread(source, base, count):
-        step = 8
-
-        def body(i, carry):
-            piece = source[pl.ds(i * step, step)].astype(F32)
-            at = pl.multiple_of(base * hc + i * step * hc, 8)
-            nope_rows[pl.ds(at, step * hc), :] = piece[:, :, :nope].reshape(step * hc, nope)
-            rope_rows[pl.ds(at, step * hc), 0:rope] = piece[:, :, nope:].reshape(step * hc, rope)
-            return carry
-
-        lax.fori_loop(0, count // step, body, 0)
-
-    spread(pq, 0, rows)
-    spread(dq, rows, samples)
 
     def absorb_head(h, carry):
-        take = pl.ds(h, rows + samples, stride=hc)
-        plain = nope_rows[take, :].astype(BF16)
+        query = pq[h].T
+        take = pl.ds(h, samples, stride=hc)
+        plain = jnp.concatenate([query[:, :nope], nope_rows[take, :].astype(BF16)], axis=0)
         turned = rope_rows[take, :].astype(BF16)
         absorbed = jnp.dot(plain, upk[h], preferred_element_type=F32).astype(BF16)
         at = pl.multiple_of(h * rows, 16)
         pre_abs[pl.ds(at, rows), 0:kv] = absorbed[:rows]
-        pre_abs[pl.ds(at, rows), kv:padded] = turned[:rows]
+        pre_abs[pl.ds(at, rows), kv : kv + rope] = query[:, nope:]
         at = pl.multiple_of(h * samples, 16)
         dec_abs[pl.ds(at, samples), 0:kv] = absorbed[rows:]
-        dec_abs[pl.ds(at, samples), kv:padded] = turned[rows:]
+        dec_abs[pl.ds(at, samples), kv:padded] = turned
         return carry
 
     pending = [functools.partial(take_z, d) for d in order]
@@ -342,7 +339,11 @@
     pre_bias[...] = jnp.where(key_at <= query_at, 0.0, MASKED)
     key_at = lax.broadcasted_iota(jnp.int32, dec_bias.shape, 1)
     own_at = prompt + lax.broadcasted_iota(jnp.int32, dec_bias.shape, 0)
-    dec_bias[...] = jnp.where((key_at < len_ref[...]) | (key_at == own_at), 0.0, MASKED)
+    diagonal = lax.broadcasted_iota(jnp.int32, (samples, samples), 0)
+    diagonal = diagonal == lax.broadcasted_iota(jnp.int32, (samples, samples), 1)
+    spread_len = jnp.broadcast_to(len_ref[...].astype(F32), (samples, samples))
+    length = jnp.sum(jnp.where(diagonal, spread_len, 0.0), axis=1, keepdims=True)
+    dec_bias[...] = jnp.where((key_at < length.astype(jnp.int32)) | (key_at == own_at), 0.0, MASKED)
 
     keys[...] = jnp.zeros_like(keys)
     keys[prompt : prompt + samples, 0:lat_width] = own_ref[...]
@@ -480,14 +481,14 @@
         in_specs=[hbm, hbm, hbm, vmem, vmem, hbm, hbm, hbm],
         out_specs=(hbm, vmem),
         scratch_shapes=[
-            pltpu.VMEM((rows, hc, width), BF16),
+            pltpu.VMEM((hc, width, rows), BF16),
             pltpu.VMEM((samples, hc, width), BF16),
             pltpu.VMEM((ns * nh, block, lat_width), BF16),
             pltpu.VMEM((hc, nope, kv), BF16),
             pltpu.VMEM((hc, kv, vdim), BF16),
             pltpu.VMEM(proj.shape, BF16),
-            pltpu.VMEM(((rows + samples) * hc, nope), F32),
-            pltpu.VMEM(((rows + samples) * hc, LANES), F32),
+            pltpu.VMEM((samples * hc, nope), F32),
+            pltpu.VMEM((samples * hc, LANES), F32),
             pltpu.VMEM((rows * hc, padded), BF16),
             pltpu.VMEM((samples * hc, padded), BF16),
             pltpu.VMEM((keys_rows, padded), BF16),
@@ -520,7 +521,7 @@
             collective_id=0, has_side_effects=True, vmem_limit_bytes=62 * 1024 * 1024
         ),
         name="rollout_step",
-    )(pq, lat, dq, own, length.reshape(samples, 1), upk, upv, proj)
+    )(jnp.transpose(pq, (1, 2, 0)), lat, dq, own, length.reshape(1, samples), upk, upv, proj)
 
 
 def per_device(ns, nh, *args):

time: 65.6 us -> 59.3 us (0.904)
  local copies, waits for them, and re-layouts: 9.7 us -> 3.84 us
    unnamed x3 -> x2, local copies, waits for them, and re-layouts: 8.36 us -> 3.84 us
    reshape x1 -> x0, local copies, waits for them, and re-layouts: 1.34 us -> none  [fused_device(): length.reshape(samples, 1)]
where the time goes in v2:
time: 59.3 us; the launch traced here: 59 us
  Pallas kernels  54.6 us (92%)
  local copies, waits for them, and re-layouts  3.84 us (6%)
  between operations  0.64 us (1%)
    pallas_call x1, Pallas kernels, fused_device(): pl.pallas_call(functools.partial(step_kernel, cfg), out_shape=(jax.ShapeD...  54.6 us
    unnamed x2, local copies, waits for them, and re-layouts  3.84 us

profile of v2, /device:TPU:0, one launch (start us, length us, event | category | flops | bytes accessed | tf_op | source)
XLA Modules:
  0.0 59.0 jit_solution(14757461660982465863)
XLA Ops:
  0.6 54.6 %rollout_step.1 = (bf16[128,4096]{1,0:T(8,128)(2,1)}, bf16[32,1792]{1,0:T(8,128)(2,1)}) custom-call(bf16[32,192,128]{2,1,0:T(8,128)(2,1)} %bitcast.2, bf16[32,576]{1,0:T(8,128)(2,1)} %lat_hbm.1, bf16[32,32,192]{2,1,0:T(8,128)(2,1)} %dq_hbm.1, bf16[32,576]{1,0:T(8,128)(2,1)} %own_ref.1, s32[1,32]{1,0:T(1,128)} %bitcast.3, bf16[32,128,512]{2,1,0:T(8,128)(2,1)} %upk_hbm.1, ...), custom_call_target="tpu_custom_call" | custom-call | tf_op jit(solution)/shard_map/rollout_step/pallas_call | solution.py:475
  55.2 2.3 %copy.12 = bf16[128,4096]{1,0:T(8,128)(2,1)} copy(bf16[128,4096]{1,0:T(8,128)(2,1)} %get-tuple-element.4) | data formatting | bytes 2097152
  57.5 1.6 %copy.13 = bf16[32,1792]{1,0:T(8,128)(2,1)} copy(bf16[32,1792]{1,0:T(8,128)(2,1)} %get-tuple-element.5) | data formatting | bytes 229376

commit v3 on v2

--- a/solution.py
+++ b/solution.py
@@ -175,6 +175,7 @@
     dec_bias,
     heads,
     out,
+    partial,
     terms,
     arrived,
     pq_sem,
@@ -357,28 +358,27 @@
 
     upv_copy.wait()
     dec_heads = cfg["dec_heads"]
-
-    def decode_group(g, carry):
-        at = pl.multiple_of(g * dec_heads * samples, 16)
+    parts = hc // dec_heads
+
+    for g in range(parts):
+        at = g * dec_heads * samples
         latent = softmax_latent(
-            dec_abs[pl.ds(at, dec_heads * samples), :],
+            dec_abs[at : at + dec_heads * samples, :],
             keys_t[...],
             keys[:, 0:kv],
             dec_bias[...],
             scale,
         )
         for i in range(dec_heads):
-            h = g * dec_heads + i
             one = jnp.dot(
-                latent[i * samples : (i + 1) * samples], upv[h], preferred_element_type=F32
+                latent[i * samples : (i + 1) * samples],
+                upv[g * dec_heads + i],
+                preferred_element_type=F32,
             )
-            heads[z, :, pl.ds(pl.multiple_of(h * vdim, vdim), vdim)] = one.astype(BF16)
-        return carry
-
-    lax.fori_loop(0, hc // dec_heads, decode_group, 0)
-    for d in order:
-        slot = heads.at[z]
-        send(slot, slot, h_send.at[d], h_recv.at[d], {"seq": seq_peer(d)})
+            heads[g, z, :, i * vdim : (i + 1) * vdim] = one.astype(BF16)
+        slot = heads.at[g, z]
+        for d in order[::-1]:
+            send(slot, slot, h_send.at[g, d], h_recv.at[g, d], {"seq": seq_peer(d)})
 
     pre_heads = cfg["pre_heads"]
     groups = hc // pre_heads
@@ -399,7 +399,7 @@
             out[:, pl.ds(pl.multiple_of(h * vdim, vdim), vdim)] = one.astype(BF16)
         return carry
 
-    first = groups // 2
+    first = groups - 1
     half_cols = first * group_cols
     lax.fori_loop(0, first, prefill_group, 0)
     front = pltpu.make_async_copy(
@@ -408,24 +408,43 @@
     front.start()
 
     proj_copy.wait()
-    for d in order:
-        at = lax.rem(z - d + ns, ns)
-        received(heads.at[at], h_recv.at[d], h_send.at[d], {"seq": seq_peer(d)})
     cols = proj.shape[1]
-    tile = cfg["tile"]
+    tile = terms.shape[3]
+    tiles = cols // tile
     share_rows = ns * samples // nh
-
-    def project(n, carry):
-        take = pl.ds(pl.multiple_of(n * tile, tile), tile)
-        left = heads[...].reshape(ns * samples, hc * vdim)
-        term = jnp.dot(left, proj[:, take], preferred_element_type=F32).astype(BF16)
-        terms[:, :, take] = term.reshape(nh, share_rows, tile)
-        return carry
-
-    lax.fori_loop(0, cols // tile, project, 0)
-    for d in range(1, nh):
-        peer = head_peer(d)
-        send(terms.at[peer], arrived.at[d], r_send.at[d], r_recv.at[d], {"head": peer})
+    depth = dec_heads * vdim
+
+    def product(g, n):
+        left = heads[g].reshape(ns * samples, depth)
+        right = proj[g * depth : (g + 1) * depth, pl.ds(pl.multiple_of(n * tile, tile), tile)]
+        return jnp.dot(left, right, preferred_element_type=F32)
+
+    for g in range(parts):
+        for d in order:
+            at = lax.rem(z - d + ns, ns)
+            received(heads.at[g, at], h_recv.at[g, d], h_send.at[g, d], {"seq": seq_peer(d)})
+        if g < parts - 1:
+
+            def project(n, carry, g=g):
+                value = product(g, n)
+                partial[n] = value if g == 0 else partial[n] + value
+                return carry
+
+            lax.fori_loop(0, tiles, project, 0)
+    for n in range(tiles):
+        value = product(parts - 1, n)
+        if parts > 1:
+            value = partial[n] + value
+        terms[n] = value.astype(BF16).reshape(nh, share_rows, tile)
+        for d in range(1, nh):
+            peer = head_peer(d)
+            send(
+                terms.at[n, peer],
+                arrived.at[n, d],
+                r_send.at[n, d],
+                r_recv.at[n, d],
+                {"head": peer},
+            )
 
     lax.fori_loop(first, groups, prefill_group, 0)
     back_cols = out.shape[1] - half_cols
@@ -435,11 +454,14 @@
         out_sem.at[1],
     )
     back.start()
-    total = terms[hd].astype(F32)
-    for d in range(1, nh):
-        received(arrived.at[d], r_recv.at[d], r_send.at[d], {"head": core_peer})
-        total = total + arrived[d].astype(F32)
-    dec_ref[...] = total.astype(BF16)
+    for n in range(tiles):
+        total = terms[n, hd].astype(F32)
+        for d in range(1, nh):
+            received(
+                arrived.at[n, d], r_recv.at[n, d], r_send.at[n, d], {"head": core_peer}
+            )
+            total = total + arrived[n, d].astype(F32)
+        dec_ref[:, n * tile : (n + 1) * tile] = total.astype(BF16)
     front.wait()
     back.wait()
     for copy in sent:
@@ -458,7 +480,10 @@
     share_rows = ns * samples // nh
     keys_rows = prompt + round_up(samples, LANES)
     nx = nh // 2
-    dec_heads = max(1, min(hc, 512 // samples))
+    dec_heads = max(1, min(hc, 256 // samples))
+    parts = hc // dec_heads
+    tile = 256 if cols % 256 == 0 else LANES
+    tiles = cols // tile
     pre_heads = max(1, min(hc // 2, 512 // rows))
     cfg = {
         "ns": ns,
@@ -467,7 +492,6 @@
         "chunks": 4,
         "dec_heads": dec_heads,
         "pre_heads": pre_heads,
-        "tile": 256 if cols % 256 == 0 else LANES,
     }
     hbm = pl.BlockSpec(memory_space=pl.ANY)
     vmem = pl.BlockSpec(memory_space=pltpu.VMEM)
@@ -495,10 +519,11 @@
             pltpu.VMEM((padded, keys_rows), BF16),
             pltpu.VMEM((rows, prompt), F32),
             pltpu.VMEM((samples, keys_rows), F32),
-            pltpu.VMEM((ns, samples, hc * vdim), BF16),
+            pltpu.VMEM((parts, ns, samples, dec_heads * vdim), BF16),
             pltpu.VMEM((rows, hc * vdim), BF16),
-            pltpu.VMEM((nh, share_rows, cols), BF16),
-            pltpu.VMEM((nh, share_rows, cols), BF16),
+            pltpu.VMEM((tiles, ns * samples, tile), F32),
+            pltpu.VMEM((tiles, nh, share_rows, tile), BF16),
+            pltpu.VMEM((tiles, nh, share_rows, tile), BF16),
             dma,
             dma,
             dma,
@@ -512,10 +537,10 @@
             dma((ns, nx)),
             dma((ns, nx)),
             dma((ns, nx)),
-            dma((ns,)),
-            dma((ns,)),
-            dma((nh,)),
-            dma((nh,)),
+            dma((parts, ns)),
+            dma((parts, ns)),
+            dma((tiles, nh)),
+            dma((tiles, nh)),
         ],
         compiler_params=pltpu.CompilerParams(
             collective_id=0, has_side_effects=True, vmem_limit_bytes=62 * 1024 * 1024
@@ -532,6 +557,7 @@
         and nh % 2 == 0
         and ns > 1
         and hc % 8 == 0
+        and hc % max(1, 256 // samples) == 0
         and pq.shape[0] % 16 == 0
         and samples % 16 == 0
         and (ns * samples) % (nh * 16) == 0

time: 59.3 us -> 53.2 us (0.90)
  Pallas kernels: 54.6 us -> 48.5 us
    pallas_call x1, Pallas kernels: 54.6 us -> 48.5 us  [fused_device(): pl.pallas_call(functools.partial(step_kernel, cfg), out_shape=(jax.ShapeD...]
where the time goes in v3:
time: 53.2 us; the launch traced here: 53 us
  Pallas kernels  48.5 us (91%)
  local copies, waits for them, and re-layouts  3.84 us (7%)
  between operations  0.64 us (1%)
    pallas_call x1, Pallas kernels, fused_device(): pl.pallas_call(functools.partial(step_kernel, cfg), out_shape=(jax.ShapeD...  48.5 us
    unnamed x2, local copies, waits for them, and re-layouts  3.84 us

profile of v3, /device:TPU:0, one launch (start us, length us, event | category | flops | bytes accessed | tf_op | source)
XLA Modules:
  0.0 53.0 jit_solution(10587226985470736352)
XLA Ops:
  0.6 48.5 %rollout_step.1 = (bf16[128,4096]{1,0:T(8,128)(2,1)}, bf16[32,1792]{1,0:T(8,128)(2,1)}) custom-call(bf16[32,192,128]{2,1,0:T(8,128)(2,1)} %bitcast.2, bf16[32,576]{1,0:T(8,128)(2,1)} %lat_hbm.1, bf16[32,32,192]{2,1,0:T(8,128)(2,1)} %dq_hbm.1, bf16[32,576]{1,0:T(8,128)(2,1)} %own_ref.1, s32[1,32]{1,0:T(1,128)} %bitcast.3, bf16[32,128,512]{2,1,0:T(8,128)(2,1)} %upk_hbm.1, ...), custom_call_target="tpu_custom_call" | custom-call | tf_op jit(solution)/shard_map/rollout_step/pallas_call | solution.py:499
  49.1 2.3 %copy.12 = bf16[128,4096]{1,0:T(8,128)(2,1)} copy(bf16[128,4096]{1,0:T(8,128)(2,1)} %get-tuple-element.4) | data formatting | bytes 2097152
  51.4 1.6 %copy.13 = bf16[32,1792]{1,0:T(8,128)(2,1)} copy(bf16[32,1792]{1,0:T(8,128)(2,1)} %get-tuple-element.5) | data formatting | bytes 229376

commit v4 on v3

--- a/solution.py
+++ b/solution.py
@@ -436,15 +436,28 @@
         if parts > 1:
             value = partial[n] + value
         terms[n] = value.astype(BF16).reshape(nh, share_rows, tile)
-        for d in range(1, nh):
-            peer = head_peer(d)
+        for j in range(nx):
             send(
-                terms.at[n, peer],
-                arrived.at[n, d],
-                r_send.at[n, d],
-                r_recv.at[n, d],
-                {"head": peer},
+                terms.at[n, lax.rem(core_peer + 2 * j, nh)],
+                arrived.at[n, j],
+                r_send.at[n, j],
+                r_recv.at[n, j],
+                {"head": core_peer},
             )
+    for n in range(tiles):
+        for j in range(nx):
+            received(arrived.at[n, j], r_recv.at[n, j], r_send.at[n, j], {"head": core_peer})
+            if j > 0:
+                peer = head_peer(2 * j)
+                pair = terms[n, peer].astype(F32) + arrived[n, j].astype(F32)
+                terms[n, peer] = pair.astype(BF16)
+                send(
+                    terms.at[n, peer],
+                    arrived.at[n, nx + j],
+                    r_send.at[n, nx + j],
+                    r_recv.at[n, nx + j],
+                    {"head": peer},
+                )
 
     lax.fori_loop(first, groups, prefill_group, 0)
     back_cols = out.shape[1] - half_cols
@@ -455,11 +468,9 @@
     )
     back.start()
     for n in range(tiles):
-        total = terms[n, hd].astype(F32)
-        for d in range(1, nh):
-            received(
-                arrived.at[n, d], r_recv.at[n, d], r_send.at[n, d], {"head": core_peer}
-            )
+        total = terms[n, hd].astype(F32) + arrived[n, 0].astype(F32)
+        for d in range(nx + 1, nh):
+            received(arrived.at[n, d], r_recv.at[n, d], r_send.at[n, d], {"head": core_peer})
             total = total + arrived[n, d].astype(F32)
         dec_ref[:, n * tile : (n + 1) * tile] = total.astype(BF16)
     front.wait()

time: 53.2 us -> 53.8 us (1.011)
  no operation moved by 1% of the time
where the time goes in v4:
time: 53.8 us; the launch traced here: 53.5 us
  Pallas kernels  49 us (91%)
  local copies, waits for them, and re-layouts  3.84 us (7%)
  between operations  0.64 us (1%)
    pallas_call x1, Pallas kernels, fused_device(): pl.pallas_call(functools.partial(step_kernel, cfg), out_shape=(jax.ShapeD...  49 us
    unnamed x2, local copies, waits for them, and re-layouts  3.84 us

profile of v4, /device:TPU:0, one launch (start us, length us, event | category | flops | bytes accessed | tf_op | source)
XLA Modules:
  0.0 53.5 jit_solution(7540983525765669706)
XLA Ops:
  0.6 49.0 %rollout_step.1 = (bf16[128,4096]{1,0:T(8,128)(2,1)}, bf16[32,1792]{1,0:T(8,128)(2,1)}) custom-call(bf16[32,192,128]{2,1,0:T(8,128)(2,1)} %bitcast.2, bf16[32,576]{1,0:T(8,128)(2,1)} %lat_hbm.1, bf16[32,32,192]{2,1,0:T(8,128)(2,1)} %dq_hbm.1, bf16[32,576]{1,0:T(8,128)(2,1)} %own_ref.1, s32[1,32]{1,0:T(1,128)} %bitcast.3, bf16[32,128,512]{2,1,0:T(8,128)(2,1)} %upk_hbm.1, ...), custom_call_target="tpu_custom_call" | custom-call | tf_op jit(solution)/shard_map/rollout_step/pallas_call | solution.py:510
  49.7 2.3 %copy.12 = bf16[128,4096]{1,0:T(8,128)(2,1)} copy(bf16[128,4096]{1,0:T(8,128)(2,1)} %get-tuple-element.4) | data formatting | bytes 2097152
  52.0 1.6 %copy.13 = bf16[32,1792]{1,0:T(8,128)(2,1)} copy(bf16[32,1792]{1,0:T(8,128)(2,1)} %get-tuple-element.5) | data formatting | bytes 229376
